TPU v7x, 32 devices: a whole 2x2x4 slice. The times are simulated.
32 devices in a mesh: groups: 2 (over y), seq: 4 (over z), mp: 2 (over x), enc: 2 (over core).
Axes of the slice: x: 2, y: 2, z: 4, core: 2. Of those that a mesh axis runs over, the one named last changes fastest.
Arguments:
- tokens: bfloat16 [4096, 4096], P(('groups', 'seq'), ('mp', 'enc')), parts along dimension 0, may hold values from -6 to 6
- nbr_feats: bfloat16 [192, 128, 4096], P(('groups', 'seq'), None, ('mp', 'enc')), parts along dimension 0, may hold values from -6 to 6
- counts: int32 [8], P('groups'), parts along dimension 0, may hold values from 8 to 24, as said below
- slot_target: int32 [192], P(('groups', 'seq')), parts along dimension 0, may hold values from 0 to 63, as said below
- w_query: bfloat16 [4096, 512], P(None, ('mp', 'enc')), may hold values from -32 to 32
- w_keyval: bfloat16 [4096, 512], P(None, ('mp', 'enc')), may hold values from -1 to 1
Outputs:
- attended: bfloat16 [4096, 512], P(('groups', 'seq'), ('mp', 'enc')), parts along dimension 0
There are 2 independent parts, one for each index of `groups`. A program takes and returns all parts, laid end to end along the dimension named above; an argument that names none is the same for every part. Nothing has to cross between parts.
Inputs may be any that keep to these rules, and one draw needn't show every extreme that they name: Each seq index's live slots are its first counts slots; the counts sum to 64. `slot_target`: A live slot holds neighbour o * 16 + l of the spans of seq index o; every neighbour is held by exactly one live slot; the live slots of one seq index hold at most 8 neighbours of any one seq index; dead slots hold arbitrary values of the range.
All inputs are finite; a program needn't handle non-finite values.
Results may differ from a plain program's by a relative error of at most 0.003.
The roundings to bfloat16 on the way count: a program that leaves them out, or rounds other values in their place, can miss the bound.
Values may be sent and summed in bfloat16 or wider, within the bound.
A program may use at most 128 MiB of HBM per device.

v0:
```python
import jax
import jax.numpy as jnp
from jax import lax
from jax.sharding import PartitionSpec as P

D = 4096
SPAN = 64
NBR = 2
RLEN = 128
CH_SEQ = 8
NB_SEQ = 16
ENC_CAP = 24


epsilon = 1e-05


def partner_2(block, axis, stride):
    count = lax.axis_size(axis)
    route = []
    for low in range(count):
        high = low | 1 << stride
        if high != low and high < count:
            route += [(low, high), (high, low)]
    return lax.ppermute(block, axis, route)


def passed_along(block, axis, distance):
    devices = range(lax.axis_size(axis))
    route = [(i - distance, i) for i in devices if i - distance in devices]
    return lax.ppermute(block, axis, route)


def project_fold(weight, piece):
    width = piece.shape[-1]
    flat_rows = piece.reshape(-1, width)
    running = jnp.dot(flat_rows, weight, preferred_element_type=jnp.float32)
    widened = flat_rows.astype(jnp.float32)
    squares = jnp.sum(widened * widened, axis=1)
    return (running, squares)


def normalized(carry, factor):
    running, squares = carry
    scale_rows = lax.rsqrt(squares / D + epsilon) * factor
    return (running * scale_rows[:, None]).astype(jnp.bfloat16)


def routing_plan(slot_target, counts, pair_cap):
    seq_count = counts.shape[0]
    seq_here = lax.axis_index("seq")
    live_count = jnp.sum(jnp.where(jnp.arange(seq_count) == seq_here, counts, 0))
    slot_ids = jnp.arange(ENC_CAP)
    live_slots = slot_ids < live_count
    owner_of = slot_target // NB_SEQ
    position = slot_target % NB_SEQ
    same_owner = (
        (owner_of[:, None] == owner_of[None, :])
        & live_slots[None, :]
        & (slot_ids[None, :] < slot_ids[:, None])
    )
    rank_within = jnp.sum(same_owner.astype(jnp.int32), axis=1)
    target_slot = owner_of * pair_cap + rank_within
    buffer_ids = jnp.arange(seq_count * pair_cap)
    chosen = (buffer_ids[:, None] == target_slot[None, :]) & live_slots[None, :]
    sent_ids = jnp.sum(jnp.where(chosen, position[None, :] + 1, 0), axis=1) - 1
    return (chosen, sent_ids.reshape(seq_count, pair_cap))


def pack_rows(chosen, payload, seq_count, pair_cap):
    packed = jnp.dot(chosen.astype(jnp.bfloat16), payload, preferred_element_type=jnp.float32)
    return packed.astype(jnp.bfloat16).reshape(seq_count, pair_cap, payload.shape[1])


def place_rows(received, received_ids):
    flat_rows = received.reshape(-1, received.shape[-1])
    picker = received_ids.reshape(1, -1) == jnp.arange(NB_SEQ)[:, None]
    placed = jnp.dot(picker.astype(jnp.bfloat16), flat_rows, preferred_element_type=jnp.float32)
    return placed.astype(jnp.bfloat16)


def local(tokens, nbr_feats, counts, slot_target, w_query, w_keyval):
    seq_count = lax.axis_size("seq")
    pair_cap = max(2, 2 * NB_SEQ // seq_count)
    head_size = w_keyval.shape[1]
    chosen, sent_ids = routing_plan(slot_target, counts, pair_cap)
    folded = project_fold(w_keyval, lax.all_gather(nbr_feats, ("mp", "enc"), axis=2, tiled=True))
    encoded = normalized(folded, 1.0).reshape(ENC_CAP, RLEN * head_size)
    packed = pack_rows(chosen, encoded, seq_count, pair_cap)
    received, received_ids = (
        lax.all_to_all(packed, "seq", split_axis=0, concat_axis=0, tiled=True),
        lax.all_to_all(sent_ids, "seq", split_axis=0, concat_axis=0, tiled=True),
    )
    own_half = place_rows(received, received_ids).reshape(NB_SEQ, RLEN, head_size)
    partner = partner_2(own_half, "enc", 0)
    first_lane = lax.axis_index("enc") == 0
    key_rows = jnp.where(first_lane, own_half, partner).reshape(CH_SEQ, NBR * RLEN, head_size)
    value_rows = jnp.where(first_lane, partner, own_half).reshape(CH_SEQ, NBR * RLEN, head_size)
    prior_keys, prior_values = passed_along((key_rows[-1], value_rows[-1]), "seq", 1)
    context_keys = jnp.concatenate([prior_keys[None], key_rows[:-1]], axis=0)
    context_values = jnp.concatenate([prior_values[None], value_rows[:-1]], axis=0)
    folded_tokens = project_fold(w_query, lax.all_gather(tokens, ("mp", "enc"), axis=1, tiled=True))
    queries = normalized(folded_tokens, head_size ** (-0.5)).reshape(CH_SEQ, SPAN, head_size)
    scores = jnp.einsum("cqd,ckd->cqk", queries, context_keys, preferred_element_type=jnp.float32)
    weights = jax.nn.softmax(scores, axis=-1).astype(jnp.bfloat16)
    attended = jnp.einsum(
        "cqk,ckd->cqd", weights, context_values, preferred_element_type=jnp.float32
    )
    return attended.astype(jnp.bfloat16).reshape(CH_SEQ * SPAN, head_size)


def solution(mesh):
    placed = (
        P(("groups", "seq"), ("mp", "enc")),
        P(("groups", "seq"), None, ("mp", "enc")),
        P("groups"),
        P(("groups", "seq")),
        P(None, ("mp", "enc")),
        P(None, ("mp", "enc")),
    )
    return jax.shard_map(
        local,
        mesh=mesh,
        in_specs=placed,
        out_specs=P(("groups", "seq"), ("mp", "enc")),
        check_vma=False,
    )
```

profile of v0, /device:TPU:16, one launch (start us, length us, event | category | flops | bytes accessed | tf_op | source)
XLA Modules:
  0.0 241.7 jit_solution(9443308790571083364)
XLA Ops:
  6.5 0.7 all-gather.5.cloned.1.call-update
  7.3 0.0 all-gather.3.cloned.1.call-start
  7.3 0.7 all-gather.3.cloned.1.call-update
  8.1 0.6 fusion.24
  8.7 0.6 iota_compare_fusion.4
  9.3 0.2 convert_reduce_fusion
  9.5 0.1 select_reduce_fusion
  9.6 0.7 sub.20
  10.3 5.2 %all-to-all-start = ((s32[4,1,8]{2,1,0:T(1,128)}), s32[4,1,8]{2,1,0:T(1,128)S(1)}, u32[]{:S(2)}, u32[]{:S(2)}) async-start(s32[4,1,8]{2,1,0:T(1,128)} %bitcast.1), calls=%async_computation | async-start | bytes 4096 | tf_op jit(solution)/shard_map/all_to_all | solution.py:92
  15.5 149.4 %all-gather.5.cloned.1.call-done = bf16[24,128,4096]{2,1,0:T(8,128)(2,1)} async-done(((bf16[24,128,1024]{2,1,0:T(8,128)(2,1)}), bf16[24,128,4096]{2,1,0:T(8,128)(2,1)}) %all-gather.5.cloned.1.call-update) | async-done | bytes 25165840 | tf_op jit(solution)/shard_map/all_gather | solution.py:87
  164.9 10.6 %multiply_reduce_fusion = f32[24,128]{1,0:T(8,128)S(1)} fusion(bf16[24,128,4096]{2,1,0:T(8,128)(2,1)} %all-gather.5.cloned.1.call-done), kind=kLoop, calls=%fused_computation.1 | loop fusion | flops 37745664 | bytes 25178112 | tf_op jit(solution)/shard_map/reduce_sum | solution.py:39
  175.6 12.0 %fusion.2 = bf16[3072,128]{1,0:T(8,128)(2,1)S(1)} fusion(bf16[3072,4096]{1,0:T(8,128)(2,1)} %bitcast.30, bf16[4096,128]{1,0:T(8,128)(2,1)S(1)} %copy-done, f32[3072]{0:T(1024)S(1)} %rsqrt_bitcast_fusion), kind=kOutput, calls=%fused_computation.7 | convolution fusion | flops 3222011904 | bytes 27013120 | tf_op jit(solution)/shard_map/dot_general | solution.py:37
  187.6 0.3 reshape.81
  188.0 1.5 fusion.1
  189.5 5.1 %all-to-all-start.1 = ((bf16[4,8,16384]{2,1,0:T(8,128)(2,1)}), bf16[4,8,16384]{2,1,0:T(8,128)(2,1)S(1)}, u32[]{:S(2)}, u32[]{:S(2)}) async-start(bf16[4,8,16384]{2,1,0:T(8,128)(2,1)} %fusion.1), calls=%async_computation.1 | async-start | bytes 2097152 | tf_op jit(solution)/shard_map/all_to_all | solution.py:91
  194.6 0.5 broadcast.93
  195.1 0.7 reduce.4
  195.8 0.1 eq.61
  195.9 21.7 %all-to-all-done.1 = bf16[4,8,16384]{2,1,0:T(8,128)(2,1)S(1)} async-done(((bf16[4,8,16384]{2,1,0:T(8,128)(2,1)}), bf16[4,8,16384]{2,1,0:T(8,128)(2,1)S(1)}, u32[]{:S(2)}, u32[]{:S(2)}) %all-to-all-start.1) | async-done | bytes 1048608 | tf_op jit(solution)/shard_map/all_to_all | solution.py:91
  217.6 0.3 fusion.4
  217.8 0.1 copy.9
  217.9 0.1 collective-permute-start
  218.0 0.0 all-gather.3.cloned.1.call-done
  218.1 3.2 %multiply_reduce_fusion.1 = f32[512]{0:T(512)S(1)} fusion(bf16[512,4096]{1,0:T(8,128)(2,1)} %all-gather.3.cloned.1.call-done), kind=kLoop, calls=%fused_computation.5 | loop fusion | flops 6290944 | bytes 4196352 | tf_op jit(solution)/shard_map/reduce_sum | solution.py:39
  221.3 0.1 broadcast_select_fusion.1
  221.5 4.3 %collective-permute-start.1 = (bf16[256,128]{1,0:T(8,128)(2,1)S(1)}, bf16[256,128]{1,0:T(8,128)(2,1)S(1)}, u32[]{:S(2)}, u32[]{:S(2)}) collective-permute-start(bf16[256,128]{1,0:T(8,128)(2,1)S(1)} %bitcast.39), channel_id=1, source_target_pairs={{0,4},{4,8},{8,12},{1,5},{5,9},{9,13},{2,6},{6,10},{10,14},{3,7},{... | collective-permute-start | bytes 196616 | tf_op jit(solution)/shard_map/ppermute | solution.py:31
  225.8 1.3 fusion.6
  227.1 1.9 collective-permute-start.2
  229.1 0.3 fusion.8
  229.4 0.5 fusion.31
  229.8 3.4 %collective-permute-done.2 = bf16[256,128]{1,0:T(8,128)(2,1)S(1)} collective-permute-done((bf16[256,128]{1,0:T(8,128)(2,1)S(1)}, bf16[256,128]{1,0:T(8,128)(2,1)S(1)}, u32[]{:S(2)}, u32[]{:S(2)}) %collective-permute-start.2) | collective-permute-done | bytes 65568 | tf_op jit(solution)/shard_map/ppermute | solution.py:31
  233.3 1.6 convolution_convert_fusion.2
  (23 shorter events, 0.2 us)
Async XLA Ops:
  6.5 169.0 %copy-start = (bf16[4096,128]{1,0:T(8,128)(2,1)S(1)}, bf16[4096,128]{1,0:T(8,128)(2,1)}, u32[]{:S(2)}) copy-start(bf16[4096,128]{1,0:T(8,128)(2,1)} %param.11) | copy-start | bytes 3145732
  6.5 1.5 copy-start.3
  6.5 1.5 copy-start.4
  6.5 158.4 %all-gather.5.cloned.1.call-start = ((), (), s32[]{:S(2)}) async-start(), calls=%async_computation.3 | async-start | bytes 31457280 | tf_op jit(solution)/shard_map/all_gather | solution.py:87
  7.3 210.8 %all-gather.3.cloned.1.call-start = ((), (), s32[]{:S(2)}) async-start(), calls=%async_computation.2 | async-start | bytes 5242880 | tf_op jit(solution)/shard_map/all_gather | solution.py:102
  10.3 179.2 %all-to-all-start = ((s32[4,1,8]{2,1,0:T(1,128)}), s32[4,1,8]{2,1,0:T(1,128)S(1)}, u32[]{:S(2)}, u32[]{:S(2)}) async-start(s32[4,1,8]{2,1,0:T(1,128)} %bitcast.1), calls=%async_computation | async-start | bytes 4096 | tf_op jit(solution)/shard_map/all_to_all | solution.py:92
  189.5 28.0 %all-to-all-start.1 = ((bf16[4,8,16384]{2,1,0:T(8,128)(2,1)}), bf16[4,8,16384]{2,1,0:T(8,128)(2,1)S(1)}, u32[]{:S(2)}, u32[]{:S(2)}) async-start(bf16[4,8,16384]{2,1,0:T(8,128)(2,1)} %fusion.1), calls=%async_computation.1 | async-start | bytes 2097152 | tf_op jit(solution)/shard_map/all_to_all | solution.py:91
  217.9 3.4 %collective-permute-start = (bf16[16,128,128]{2,1,0:T(8,128)(2,1)S(1)}, bf16[16,128,128]{2,1,0:T(8,128)(2,1)S(1)}, u32[]{:S(2)}, u32[]{:S(2)}) collective-permute-start(bf16[16,128,128]{2,1,0:T(8,128)(2,1)S(1)} %bitcast.31), channel_id=1, source_target_pairs={{0,1},{1,0},{2,3},{3,2},{4,5},{5,4},{6,7},{7,6},{8,9},{9,8},{10,11... | collective-permute-start | bytes 1572872 | tf_op jit(solution)/shard_map/ppermute | solution.py:25
  218.0 7.7 %copy-start.1 = (bf16[512,4096]{1,0:T(8,128)(2,1)S(1)}, bf16[512,4096]{1,0:T(8,128)(2,1)}, u32[]{:S(2)}) copy-start(bf16[512,4096]{1,0:T(8,128)(2,1)} %all-gather.3.cloned.1.call-done) | copy-start | bytes 12582916
  218.1 7.7 %copy-start.2 = (bf16[4096,128]{1,0:T(8,128)(2,1)S(1)}, bf16[4096,128]{1,0:T(8,128)(2,1)}, u32[]{:S(2)}) copy-start(bf16[4096,128]{1,0:T(8,128)(2,1)} %param.10) | copy-start | bytes 3145732
  221.5 7.6 %collective-permute-start.1 = (bf16[256,128]{1,0:T(8,128)(2,1)S(1)}, bf16[256,128]{1,0:T(8,128)(2,1)S(1)}, u32[]{:S(2)}, u32[]{:S(2)}) collective-permute-start(bf16[256,128]{1,0:T(8,128)(2,1)S(1)} %bitcast.39), channel_id=1, source_target_pairs={{0,4},{4,8},{8,12},{1,5},{5,9},{9,13},{2,6},{6,10},{10,14},{3,7},{... | collective-permute-start | bytes 196616 | tf_op jit(solution)/shard_map/ppermute | solution.py:31
  227.1 6.2 %collective-permute-start.2 = (bf16[256,128]{1,0:T(8,128)(2,1)S(1)}, bf16[256,128]{1,0:T(8,128)(2,1)S(1)}, u32[]{:S(2)}, u32[]{:S(2)}) collective-permute-start(bf16[256,128]{1,0:T(8,128)(2,1)S(1)} %bitcast.40), channel_id=1, source_target_pairs={{0,4},{4,8},{8,12},{1,5},{5,9},{9,13},{2,6},{6,10},{10,14},{3,7},{... | collective-permute-start | bytes 196616 | tf_op jit(solution)/shard_map/ppermute | solution.py:31
Sparse Core Ops, SparseCore 0:
  8.9 155.9 all-gather.4
  166.5 34.4 all-gather.2
where the time goes:
time: 242 us
  waiting for transfers between devices  176 us (73%)
  matrix products  17.5 us (7%)
  starting transfers between devices  16.6 us (7%)
  other arithmetic  16.3 us (7%)
  between operations  13.6 us (6%)
    all_gather x1, waiting for transfers between devices, local(): lax.all_gather(nbr_feats, ('mp', 'enc'), axis=2, tiled=True)  149 us
    all_to_all x1, waiting for transfers between devices, local(): lax.all_to_all(packed, 'seq', split_axis=0, concat_axis=0, tiled=True)  21.7 us
    reduce_sum x2, other arithmetic, project_fold(): squares = jnp.sum(widened * widened, axis=1)  13.9 us
    dot_general x2, matrix products, project_fold(): running = jnp.dot(flat_rows, weight, preferred_element_type=jnp.float32)  13.3 us
    ppermute x2, starting transfers between devices, passed_along(): return lax.ppermute(block, axis, route)  6.2 us
    all_to_all x1, starting transfers between devices, local(): lax.all_to_all(sent_ids, 'seq', split_axis=0, concat_axis=0, tiled=True)  5.2 us
    all_to_all x1, starting transfers between devices, local(): lax.all_to_all(packed, 'seq', split_axis=0, concat_axis=0, tiled=True)  5.11 us
  transfers between devices with their start and end apart: 7, of which 3 were waited for; matrix products, arithmetic and copies ran while one was open for 14% of the time, Pallas kernels for 0%

commit v1 on v0

--- a/solution.py
+++ b/solution.py
@@ -34,9 +34,11 @@
 def project_fold(weight, piece):
     width = piece.shape[-1]
     flat_rows = piece.reshape(-1, width)
-    running = jnp.dot(flat_rows, weight, preferred_element_type=jnp.float32)
+    mine = lax.all_to_all(weight, ("mp", "enc"), split_axis=0, concat_axis=1, tiled=True)
+    partial = jnp.dot(flat_rows, mine, preferred_element_type=jnp.float32)
+    running = lax.psum_scatter(partial, ("mp", "enc"), scatter_dimension=1, tiled=True)
     widened = flat_rows.astype(jnp.float32)
-    squares = jnp.sum(widened * widened, axis=1)
+    squares = lax.psum(jnp.sum(widened * widened, axis=1), ("mp", "enc"))
     return (running, squares)
 
 
@@ -84,7 +86,7 @@
     pair_cap = max(2, 2 * NB_SEQ // seq_count)
     head_size = w_keyval.shape[1]
     chosen, sent_ids = routing_plan(slot_target, counts, pair_cap)
-    folded = project_fold(w_keyval, lax.all_gather(nbr_feats, ("mp", "enc"), axis=2, tiled=True))
+    folded = project_fold(w_keyval, nbr_feats)
     encoded = normalized(folded, 1.0).reshape(ENC_CAP, RLEN * head_size)
     packed = pack_rows(chosen, encoded, seq_count, pair_cap)
     received, received_ids = (
@@ -99,7 +101,7 @@
     prior_keys, prior_values = passed_along((key_rows[-1], value_rows[-1]), "seq", 1)
     context_keys = jnp.concatenate([prior_keys[None], key_rows[:-1]], axis=0)
     context_values = jnp.concatenate([prior_values[None], value_rows[:-1]], axis=0)
-    folded_tokens = project_fold(w_query, lax.all_gather(tokens, ("mp", "enc"), axis=1, tiled=True))
+    folded_tokens = project_fold(w_query, tokens)
     queries = normalized(folded_tokens, head_size ** (-0.5)).reshape(CH_SEQ, SPAN, head_size)
     scores = jnp.einsum("cqd,ckd->cqk", queries, context_keys, preferred_element_type=jnp.float32)
     weights = jax.nn.softmax(scores, axis=-1).astype(jnp.bfloat16)

time: 242 us -> 158 us (0.65)
  waiting for transfers between devices: 176 us -> 64.7 us
  blocking collectives: 0 us -> 28.1 us
  other arithmetic: 16.3 us -> 11 us
  starting transfers between devices: 16.6 us -> 20.9 us
    all_gather x2 -> x0, waiting for transfers between devices: 149 us -> none  [the longest x1 149 us: local(): lax.all_gather(nbr_feats, ('mp', 'enc'), axis=2, tiled=True)]
    reduce_scatter x0 -> x2, waiting for transfers between devices: none -> 42.5 us  [project_fold(): lax.psum_scatter(partial, ('mp', 'enc'), scatter_dimension=1, tiled=True)]
    all_to_all x0 -> x1, blocking collectives: none -> 17.9 us  [project_fold(): lax.all_to_all(weight, ('mp', 'enc'), split_axis=0, concat_axis=1, tiled=...]
    psum x0 -> x1, blocking collectives: none -> 10.1 us  [project_fold(): squares = lax.psum(jnp.sum(widened * widened, axis=1), ('mp', 'enc'))]
    reduce_sum x2, other arithmetic: 13.9 us -> 5.68 us  [project_fold(): squares = lax.psum(jnp.sum(widened * widened, axis=1), ('mp', 'enc'))]
    all_to_all x1, waiting for transfers between devices: 21.7 us -> 17.6 us  [local(): lax.all_to_all(packed, 'seq', split_axis=0, concat_axis=0, tiled=True)]
    all_to_all x0 -> x1, starting transfers between devices: none -> 3.53 us  [project_fold(): lax.all_to_all(weight, ('mp', 'enc'), split_axis=0, concat_axis=1, tiled=...]
    convert_element_type x0 -> x2, other arithmetic: none -> 2.95 us  [normalized(): return (running * scale_rows[:, None]).astype(jnp.bfloat16)]
  transfers between devices with their start and end apart: 7 -> 8, of which waited for: 3 -> 4; matrix products, arithmetic and copies ran while one was open for 14% -> 12% of each run, Pallas kernels for 0% -> 0%
where the time goes in v1:
time: 158 us; the launch traced here: 157 us
  waiting for transfers between devices  64.7 us (41%)
  blocking collectives  28.1 us (18%)
  starting transfers between devices  20.9 us (13%)
  matrix products  15.5 us (10%)
  between operations  13.6 us (9%)
  other arithmetic  11 us (7%)
  local copies, waits for them, and re-layouts  3.44 us (2%)
    reduce_scatter x2, waiting for transfers between devices, project_fold(): lax.psum_scatter(partial, ('mp', 'enc'), scatter_dimension=1, tiled=True)  42.5 us
    all_to_all x1, blocking collectives, project_fold(): lax.all_to_all(weight, ('mp', 'enc'), split_axis=0, concat_axis=1, tiled=...  17.9 us
    all_to_all x1, waiting for transfers between devices, local(): lax.all_to_all(packed, 'seq', split_axis=0, concat_axis=0, tiled=True)  17.6 us
    dot_general x2, matrix products, project_fold(): partial = jnp.dot(flat_rows, mine, preferred_element_type=jnp.float32)  11.3 us
    psum x1, blocking collectives, project_fold(): squares = lax.psum(jnp.sum(widened * widened, axis=1), ('mp', 'enc'))  10.1 us
    ppermute x2, starting transfers between devices, passed_along(): return lax.ppermute(block, axis, route)  6.97 us
    reduce_sum x2, other arithmetic, project_fold(): squares = lax.psum(jnp.sum(widened * widened, axis=1), ('mp', 'enc'))  5.68 us
    all_to_all x1, starting transfers between devices, local(): lax.all_to_all(sent_ids, 'seq', split_axis=0, concat_axis=0, tiled=True)  5.21 us
  transfers between devices with their start and end apart: 8, of which 4 were waited for; matrix products, arithmetic and copies ran while one was open for 12% of the time, Pallas kernels for 0%

profile of v1, /device:TPU:16, one launch (start us, length us, event | category | flops | bytes accessed | tf_op | source)
XLA Modules:
  0.0 157.2 jit_solution(10711013462824801652)
XLA Ops:
  6.5 17.9 %all_to_all.49 = bf16[4,1024,128]{2,1,0:T(8,128)(2,1)S(1)} all-to-all(bf16[4,1024,128]{2,1,0:T(8,128)(2,1)} %bitcast.41), channel_id=1, replica_groups=mesh['groups'=2,'seq'=4,'mp'=2,'enc'=2] {'mp','enc'}, dimensions={0} | all-to-all | bytes 2097152 | tf_op jit(solution)/shard_map/all_to_all | solution.py:37
  24.5 0.5 copy.14
  25.0 8.2 %fusion.33 = f32[3072,512]{1,0:T(8,128)} fusion(bf16[3072,1024]{1,0:T(8,128)(2,1)} %bitcast.35, bf16[1024,512]{0,1:T(8,128)(2,1)S(1)} %bitcast.42), kind=kOutput, calls=%fused_computation.53 | convolution fusion | flops 3221225472 | bytes 13631488 | tf_op jit(solution)/shard_map/dot_general | solution.py:38
  33.3 0.6 copy-done.1
  33.9 0.6 fusion.22
  34.6 0.6 iota_compare_fusion.4
  35.2 0.2 convert_reduce_fusion
  35.5 0.7 sub.20
  36.2 5.2 %all-to-all-start.1 = ((s32[4,1,8]{2,1,0:T(1,128)}), s32[4,1,8]{2,1,0:T(1,128)S(1)}, u32[]{:S(2)}, u32[]{:S(2)}) async-start(s32[4,1,8]{2,1,0:T(1,128)} %bitcast.4), calls=%async_computation.2 | async-start | bytes 4096 | tf_op jit(solution)/shard_map/all_to_all | solution.py:94
  41.4 0.3 multiply_reduce_fusion.1
  41.7 5.4 %multiply_reduce_fusion = f32[24,128]{1,0:T(8,128)S(1)} fusion(bf16[24,128,1024]{2,1,0:T(8,128)(2,1)} %param.7), kind=kLoop, calls=%fused_computation.4 | loop fusion | flops 9434112 | bytes 6303744 | tf_op jit(solution)/shard_map/reduce_sum | solution.py:41
  47.1 10.1 %all-reduce = (f32[3072]{0:T(1024)S(1)}, f32[512]{0:T(512)S(1)}) all-reduce(f32[3072]{0:T(1024)S(1)} %bitcast.51, f32[512]{0:T(512)S(1)} %multiply_reduce_fusion.1), channel_id=1, replica_groups=mesh['groups'=2,'seq'=4,'mp'=2,'enc'=2] {'mp','enc'}, use_global_device_ids=true, to_apply=%region_8.9 | all-reduce | flops 3584 | bytes 28672 | tf_op jit(solution)/shard_map/psum | solution.py:41
  57.3 3.5 %all-to-all-start = ((bf16[4,1024,128]{2,1,0:T(8,128)(2,1)}), bf16[4,1024,128]{2,1,0:T(8,128)(2,1)S(1)}, u32[]{:S(2)}, u32[]{:S(2)}) async-start(bf16[4,1024,128]{2,1,0:T(8,128)(2,1)} %bitcast), calls=%async_computation | async-start | bytes 2097152 | tf_op jit(solution)/shard_map/all_to_all | solution.py:37
  60.8 42.4 %reduce-scatter.5.cloned.1.call-done = f32[3072,128]{1,0:T(8,128)} async-done(((f32[3072,512]{1,0:T(8,128)}), f32[3072,128]{1,0:T(8,128)}) %reduce-scatter.5.cloned.1.call-update) | async-done | bytes 1572880 | tf_op jit(solution)/shard_map/reduce_scatter | solution.py:39
  103.2 1.9 %multiply_convert_fusion = bf16[3072,128]{1,0:T(8,128)(2,1)S(1)} fusion(f32[3072,128]{1,0:T(8,128)} %reduce-scatter.5.cloned.1.call-done, f32[3072]{0:T(1024)S(1)} %add_rsqrt_fusion), kind=kLoop, calls=%fused_computation.6 | loop fusion | flops 786432 | bytes 2371584 | tf_op jit(solution)/shard_map/convert_element_type | solution.py:48
  105.1 0.3 reshape.70
  105.5 1.5 fusion.1
  107.0 5.1 %all-to-all-start.3 = ((bf16[4,8,16384]{2,1,0:T(8,128)(2,1)}), bf16[4,8,16384]{2,1,0:T(8,128)(2,1)S(1)}, u32[]{:S(2)}, u32[]{:S(2)}) async-start(bf16[4,8,16384]{2,1,0:T(8,128)(2,1)} %fusion.1), calls=%async_computation.5 | async-start | bytes 2097152 | tf_op jit(solution)/shard_map/all_to_all | solution.py:93
  112.1 0.5 copy.12
  112.7 3.0 %fusion.32 = f32[512,512]{1,0:T(8,128)} fusion(bf16[512,1024]{1,0:T(8,128)(2,1)} %param.6, bf16[1024,512]{0,1:T(8,128)(2,1)S(1)} %bitcast.43), kind=kOutput, calls=%fused_computation.52 | convolution fusion | flops 536870912 | bytes 3145728 | tf_op jit(solution)/shard_map/dot_general | solution.py:38
  115.7 0.5 broadcast.71
  116.2 0.7 reduce.4
  116.9 17.6 %all-to-all-done.3 = bf16[4,8,16384]{2,1,0:T(8,128)(2,1)S(1)} async-done(((bf16[4,8,16384]{2,1,0:T(8,128)(2,1)}), bf16[4,8,16384]{2,1,0:T(8,128)(2,1)S(1)}, u32[]{:S(2)}, u32[]{:S(2)}) %all-to-all-start.3) | async-done | bytes 1048608 | tf_op jit(solution)/shard_map/all_to_all | solution.py:93
  134.6 0.3 fusion.3
  135.1 1.9 %collective-permute-done = bf16[16,128,128]{2,1,0:T(8,128)(2,1)S(1)} collective-permute-done((bf16[16,128,128]{2,1,0:T(8,128)(2,1)S(1)}, bf16[16,128,128]{2,1,0:T(8,128)(2,1)S(1)}, u32[]{:S(2)}, u32[]{:S(2)}) %collective-permute-start) | collective-permute-done | bytes 524320 | tf_op jit(solution)/shard_map/ppermute | solution.py:25
  137.1 4.3 %collective-permute-start.1 = (bf16[256,128]{1,0:T(8,128)(2,1)S(1)}, bf16[256,128]{1,0:T(8,128)(2,1)S(1)}, u32[]{:S(2)}, u32[]{:S(2)}) collective-permute-start(bf16[256,128]{1,0:T(8,128)(2,1)S(1)} %bitcast.49), channel_id=1, source_target_pairs={{0,4},{4,8},{8,12},{1,5},{5,9},{9,13},{2,6},{6,10},{10,14},{3,7},{... | collective-permute-start | bytes 196616 | tf_op jit(solution)/shard_map/ppermute | solution.py:31
  141.4 1.1 multiply_convert_fusion.1
  142.6 2.7 %collective-permute-start.2 = (bf16[256,128]{1,0:T(8,128)(2,1)S(1)}, bf16[256,128]{1,0:T(8,128)(2,1)S(1)}, u32[]{:S(2)}, u32[]{:S(2)}) collective-permute-start(bf16[256,128]{1,0:T(8,128)(2,1)S(1)} %bitcast.50), channel_id=1, source_target_pairs={{0,4},{4,8},{8,12},{1,5},{5,9},{9,13},{2,6},{6,10},{10,14},{3,7},{... | collective-permute-start | bytes 196616 | tf_op jit(solution)/shard_map/ppermute | solution.py:31
  145.3 0.3 fusion.6
  145.6 0.5 fusion.29
  146.0 2.7 %collective-permute-done.2 = bf16[256,128]{1,0:T(8,128)(2,1)S(1)} collective-permute-done((bf16[256,128]{1,0:T(8,128)(2,1)S(1)}, bf16[256,128]{1,0:T(8,128)(2,1)S(1)}, u32[]{:S(2)}, u32[]{:S(2)}) %collective-permute-start.2) | collective-permute-done | bytes 65568 | tf_op jit(solution)/shard_map/ppermute | solution.py:31
  148.7 1.6 %convolution_convert_fusion.2 = bf16[8,64,128]{2,1,0:T(8,128)(2,1)} fusion(bf16[7,256,128]{2,1,0:T(8,128)(2,1)S(1)} %bitcast.46, bf16[1,256,128]{2,1,0:T(8,128)(2,1)S(1)} %bitcast.52, f32[8,64]{1,0:T(8,128)S(1)} %fusion.29, f32[8,64,256]{2,1,0:T(8,128)S(1)} %fusion.6), kind=kOutput, calls=%fused_computation.10 | convolution fusion | flops 34276096 | bytes 1181696 | tf_op jit(solution)/shard_map/cqk,ckd->cqd/dot_general | solution.py:108
  (27 shorter events, 0.6 us)
Async XLA Ops:
  6.5 96.7 %reduce-scatter.5.cloned.1.call-start = ((), (), s32[]{:S(2)}) async-start(), calls=%async_computation.7 | async-start | bytes 7864320 | tf_op jit(solution)/shard_map/reduce_scatter | solution.py:39
  33.3 0.7 copy-start.1
  33.3 1.9 %copy-start.2 = (s32[24]{0:T(128)S(1)}, s32[24]{0:T(128)}, u32[]{:S(2)}) copy-start(s32[24]{0:T(128)} %param.9) | copy-start | bytes 292
  33.3 8.1 %copy-start = (bf16[512,1024]{1,0:T(8,128)(2,1)S(1)}, bf16[512,1024]{1,0:T(8,128)(2,1)}, u32[]{:S(2)}) copy-start(bf16[512,1024]{1,0:T(8,128)(2,1)} %param.6) | copy-start | bytes 3145732
  36.2 21.1 %all-to-all-start.1 = ((s32[4,1,8]{2,1,0:T(1,128)}), s32[4,1,8]{2,1,0:T(1,128)S(1)}, u32[]{:S(2)}, u32[]{:S(2)}) async-start(s32[4,1,8]{2,1,0:T(1,128)} %bitcast.4), calls=%async_computation.2 | async-start | bytes 4096 | tf_op jit(solution)/shard_map/all_to_all | solution.py:94
  57.3 49.7 %all-to-all-start = ((bf16[4,1024,128]{2,1,0:T(8,128)(2,1)}), bf16[4,1024,128]{2,1,0:T(8,128)(2,1)S(1)}, u32[]{:S(2)}, u32[]{:S(2)}) async-start(bf16[4,1024,128]{2,1,0:T(8,128)(2,1)} %bitcast), calls=%async_computation | async-start | bytes 2097152 | tf_op jit(solution)/shard_map/all_to_all | solution.py:37
  107.0 27.6 %all-to-all-start.3 = ((bf16[4,8,16384]{2,1,0:T(8,128)(2,1)}), bf16[4,8,16384]{2,1,0:T(8,128)(2,1)S(1)}, u32[]{:S(2)}, u32[]{:S(2)}) async-start(bf16[4,8,16384]{2,1,0:T(8,128)(2,1)} %fusion.1), calls=%async_computation.5 | async-start | bytes 2097152 | tf_op jit(solution)/shard_map/all_to_all | solution.py:93
  112.1 29.2 %reduce-scatter.3.cloned.1.call-start = ((), (), s32[]{:S(2)}) async-start(), calls=%async_computation.6 | async-start | bytes 1310720 | tf_op jit(solution)/shard_map/reduce_scatter | solution.py:39
  135.0 2.0 %collective-permute-start = (bf16[16,128,128]{2,1,0:T(8,128)(2,1)S(1)}, bf16[16,128,128]{2,1,0:T(8,128)(2,1)S(1)}, u32[]{:S(2)}, u32[]{:S(2)}) collective-permute-start(bf16[16,128,128]{2,1,0:T(8,128)(2,1)S(1)} %bitcast.38), channel_id=1, source_target_pairs={{0,1},{1,0},{2,3},{3,2},{4,5},{5,4},{6,7},{7,6},{8,9},{9,8},{10,11... | collective-permute-start | bytes 1572872 | tf_op jit(solution)/shard_map/ppermute | solution.py:25
  137.1 8.2 %collective-permute-start.1 = (bf16[256,128]{1,0:T(8,128)(2,1)S(1)}, bf16[256,128]{1,0:T(8,128)(2,1)S(1)}, u32[]{:S(2)}, u32[]{:S(2)}) collective-permute-start(bf16[256,128]{1,0:T(8,128)(2,1)S(1)} %bitcast.49), channel_id=1, source_target_pairs={{0,4},{4,8},{8,12},{1,5},{5,9},{9,13},{2,6},{6,10},{10,14},{3,7},{... | collective-permute-start | bytes 196616 | tf_op jit(solution)/shard_map/ppermute | solution.py:31
  142.6 6.2 %collective-permute-start.2 = (bf16[256,128]{1,0:T(8,128)(2,1)S(1)}, bf16[256,128]{1,0:T(8,128)(2,1)S(1)}, u32[]{:S(2)}, u32[]{:S(2)}) collective-permute-start(bf16[256,128]{1,0:T(8,128)(2,1)S(1)} %bitcast.50), channel_id=1, source_target_pairs={{0,4},{4,8},{8,12},{1,5},{5,9},{9,13},{2,6},{6,10},{10,14},{3,7},{... | collective-permute-start | bytes 196616 | tf_op jit(solution)/shard_map/ppermute | solution.py:31
Sparse Core Ops, SparseCore 0:
  33.4 69.7 reduce-scatter.4
  115.8 24.8 reduce-scatter.2

commit v2 on v1

--- a/solution.py
+++ b/solution.py
@@ -1,6 +1,9 @@
+import functools
 import jax
 import jax.numpy as jnp
 from jax import lax
+from jax.experimental import pallas as pl
+from jax.experimental.pallas import tpu as pltpu
 from jax.sharding import PartitionSpec as P
 
 D = 4096
@@ -111,7 +114,398 @@
     return attended.astype(jnp.bfloat16).reshape(CH_SEQ * SPAN, head_size)
 
 
+CHUNKS = 4
+CROWS = RLEN // 2 // CHUNKS
+CFLAT = ENC_CAP * CROWS
+
+
+def fused(
+    S, cap, trow, cnt, feats, tokens, wq, wkv, out,
+    xb, tb, wown, woth, sown, ssend, srecv, town, tsend, trecv, ss, ssr,
+    enc, zs, zr, zl, ctx, qb, qs, tab, tabr, pidx_v, lidx_v, pidx, lidx,
+    lsem, send, recv,
+):
+    f32 = jnp.float32
+    g, r, m, e = (lax.axis_index(a) for a in ("groups", "seq", "mp", "enc"))
+    pg, pm, pe = 1 - g, 1 - m, 1 - e
+    K = feats.shape[2]
+    half = tokens.shape[0] // 2
+    C = CHUNKS
+    partner, across, beside = {"enc": pe}, {"mp": pm}, {"groups": pg}
+
+    ids = {}
+    total = 0
+    for name, count in (
+        ("wx", 2), ("wo", 2), ("wf", 2), ("wy", 2), ("wg", 2), ("x", C), ("t", 1), ("ss", 1),
+        ("s", C), ("ts", 1), ("tab", S), ("z", C * S), ("fwd", C), ("pr0", C), ("pr1", C), ("q", 1),
+    ):
+        ids[name] = total
+        total += count
+
+    def rc(src, dst, name, at, device):
+        i = ids[name] + at
+        return pltpu.make_async_remote_copy(
+            src_ref=src, dst_ref=dst, send_sem=send.at[i], recv_sem=recv.at[i],
+            device_id=device, device_id_type=pl.DeviceIdType.MESH,
+        )
+
+    def landed(dst, name, at, device):
+        rc(dst, dst, name, at, device).wait_recv()
+
+    def lanes(index):
+        return pl.ds(pl.multiple_of(index * 128, 128), 128)
+
+    def rows(start, size):
+        return pl.ds(pl.multiple_of(start, 16), size)
+
+    def zdev(d):
+        return {"seq": lax.rem(r + d, S)}
+
+    barrier = pltpu.get_barrier_semaphore()
+    for d in range(S):
+        for other in (False, True):
+            if d or other:
+                device = dict(zdev(d), enc=pe if other else e)
+                pl.semaphore_signal(
+                    barrier, inc=1, device_id=device, device_id_type=pl.DeviceIdType.MESH
+                )
+    for device in (across, beside):
+        pl.semaphore_signal(barrier, inc=1, device_id=device, device_id_type=pl.DeviceIdType.MESH)
+    pl.semaphore_wait(barrier, 2 * S + 1)
+
+    weights = (wkv, wq)
+    done = []
+
+    def begin(copy):
+        copy.start()
+        done.append(copy)
+
+    def piece(k, part, side):
+        return woth.at[k, rows(part * K, K), lanes(side)]
+
+    def weight_across(k):
+        begin(rc(weights[k].at[rows(2 * K * pm + K * g, K), :], piece(k, g, e), "wx", k, across))
+
+    def weight_local(k):
+        source = weights[k].at[rows(2 * K * m, 2 * K), :]
+        target = wown.at[k, :, lanes(e)]
+        begin(rc(source, target, "wo", k, partner))
+        return pltpu.make_async_copy(source, target, lsem.at[C + k])
+
+    def own_chunk(c):
+        return pltpu.make_async_copy(
+            feats.at[:, rows(CROWS * C * e + CROWS * c, CROWS), :], xb.at[e, c], lsem.at[c]
+        )
+
+    def sent_chunk(c):
+        return rc(
+            feats.at[:, rows(CROWS * C * pe + CROWS * c, CROWS), :], xb.at[e, c], "x", c, partner
+        )
+
+    weight_across(0)
+    local_kv = weight_local(0)
+    local_kv.start()
+    for c in range(C):
+        sent_chunk(c).start()
+        own_chunk(c).start()
+    weight_across(1)
+    local_q = weight_local(1)
+    local_q.start()
+    begin(rc(tokens.at[rows(half * pe, half), :], tb.at[e], "t", 0, partner))
+    local_t = pltpu.make_async_copy(tokens.at[rows(half * e, half), :], tb.at[e], lsem.at[C + 2])
+    local_t.start()
+
+    t_row = trow[...]
+    iota = lambda shape, axis: lax.broadcasted_iota(jnp.int32, shape, axis)
+    E = ENC_CAP
+    t_col = jnp.sum(jnp.where(iota((E, E), 0) == iota((E, E), 1), t_row, 0), axis=1, keepdims=True)
+    live = jnp.sum(jnp.where(iota((1, S), 1) == r, cnt[...], 0), axis=1, keepdims=True)
+    same = (
+        ((t_col >> 4) == (t_row >> 4)) & (iota((E, E), 1) < live) & (iota((E, E), 1) < iota((E, E), 0))
+    )
+    rank = jnp.sum(jnp.where(same, 1, 0), axis=1, keepdims=True)
+    at_lane = iota((E, 128), 1)
+    slot = iota((E, 128), 0)
+    is_live = slot < live
+    wanted = ((t_col >> 4) * cap + rank == at_lane) & is_live
+    source_row = jnp.sum(jnp.where(wanted, slot, 0), axis=0, keepdims=True)
+    held = (t_col == at_lane) & is_live
+    place_row = jnp.sum(jnp.where(held, r * cap + rank, 0), axis=0, keepdims=True)
+    pidx_v[...] = jnp.broadcast_to(source_row, (8, 128))
+    tab[...] = jnp.broadcast_to(place_row, (8, 128))
+    pack_copy = pltpu.make_async_copy(pidx_v, pidx, lsem.at[C + 3])
+    pack_copy.start()
+    for d in range(1, S):
+        begin(rc(tab, tabr.at[d], "tab", d, zdev(d)))
+    tabr[0] = tab[...]
+
+    ss[...] = jnp.zeros_like(ss)
+    eye = iota((128, 128), 0) == iota((128, 128), 1)
+
+    def as_rows(column):
+        blocks = column.reshape(-1, 128, 1)
+        return jnp.sum(jnp.where(eye[None], blocks, 0.0), axis=1)
+
+    def as_column(lined):
+        blocks = jnp.where(eye[None], lined[:, None, :], 0.0)
+        return jnp.sum(blocks, axis=2, keepdims=True).reshape(-1, 1)
+
+    def squares(block):
+        wide = block.astype(f32)
+        return jnp.sum(wide * wide, axis=1, keepdims=True)
+
+    def product(first, second, weight, k):
+        return jnp.dot(first, weight[k, :K, :], preferred_element_type=f32) + jnp.dot(
+            second, weight[k, K:, :], preferred_element_type=f32
+        )
+
+    def chunk_rows(c):
+        return xb[0, c].reshape(CFLAT, K), xb[1, c].reshape(CFLAT, K)
+
+    def first_pass(c, carry):
+        own_chunk(c).wait()
+        landed(xb.at[pe, c], "x", c, partner)
+        one, two = chunk_rows(c)
+        ss[c, 0 : CFLAT // 128, :] = as_rows(squares(one) + squares(two))
+        sown[c] = product(one, two, wown, 0)
+        return carry
+
+    def spread_across(k):
+        landed(piece(k, g, e), "wx", k, across)
+        begin(rc(piece(k, g, e), piece(k, g, e), "wy", k, beside))
+        begin(rc(piece(k, g, e), piece(k, g, e), "wf", k, partner))
+
+    def spread_beside(k):
+        landed(piece(k, pg, e), "wy", k, beside)
+        begin(rc(piece(k, pg, e), piece(k, pg, e), "wg", k, partner))
+
+    def spread_end(k):
+        landed(piece(k, g, pe), "wf", k, partner)
+        landed(piece(k, pg, pe), "wg", k, partner)
+
+    local_kv.wait()
+    landed(wown.at[0, :, lanes(pe)], "wo", 0, partner)
+    spread_across(0)
+    lax.fori_loop(0, C // 2, first_pass, 0)
+    spread_beside(0)
+    spread_across(1)
+    lax.fori_loop(C // 2, C, first_pass, 0)
+    local_q.wait()
+    landed(wown.at[1, :, lanes(pe)], "wo", 1, partner)
+    local_t.wait()
+    landed(tb.at[pe], "t", 0, partner)
+    ss[C, 0 : half // 128, :] = as_rows(squares(tb[0]) + squares(tb[1]))
+    begin(rc(ss, ssr, "ss", 0, across))
+    spread_beside(1)
+    spread_end(0)
+
+    def partial_copy(c):
+        return rc(ssend.at[c], srecv.at[c], "s", c, across)
+
+    def second_pass(c, carry):
+        one, two = chunk_rows(c)
+        ssend[c] = product(one, two, woth, 0)
+        partial_copy(c).start()
+        return carry
+
+    lax.fori_loop(0, C, second_pass, 0)
+    spread_end(1)
+    tsend[...] = product(tb[0], tb[1], woth, 1)
+    begin(rc(tsend, trecv, "ts", 0, across))
+    town[...] = product(tb[0], tb[1], wown, 1)
+
+    for d in range(1, S):
+        landed(tabr.at[d], "tab", d, zdev(d))
+    places = tabr[0]
+    for d in range(1, S):
+        places = places + tabr[d]
+    lidx_v[...] = places
+    place_copy = pltpu.make_async_copy(lidx_v, lidx, lsem.at[C + 4])
+    place_copy.start()
+    pack_copy.wait()
+    place_copy.wait()
+
+    @pl.when(r == 0)
+    def _():
+        ctx[0:2] = jnp.zeros((2,) + ctx.shape[1:], ctx.dtype)
+
+    def z_copy(c, d):
+        return rc(zs.at[c, lax.rem(r + d, S)], zr.at[c, r], "z", c * S + d, zdev(d))
+
+    def z_landed(c, d):
+        source = lax.rem(r + S - d, S)
+        landed(zr.at[c, source], "z", c * S + d, {"seq": source})
+
+    def ctx_rows(side, c):
+        return rows(CROWS * C * side + CROWS * c, CROWS)
+
+    def own_rows(side, c):
+        return ctx.at[pl.ds(2, NB_SEQ), ctx_rows(side, c), :]
+
+    def forward_copy(c):
+        return rc(own_rows(e, c), own_rows(e, c), "fwd", c, partner)
+
+    def prior_copy(c, same_core):
+        return rc(
+            ctx.at[pl.ds(NB_SEQ, 2), ctx_rows(e, c), :],
+            ctx.at[pl.ds(0, 2), ctx_rows(e, c), :],
+            "pr0" if same_core else "pr1", c,
+            {"seq": lax.rem(r + 1, S), "enc": e if same_core else pe},
+        )
+
+    landed(ssr, "ss", 0, across)
+
+    def factor(at, count):
+        lined = ss[at, 0:count, :] + ssr[at, 0:count, :]
+        return lax.rsqrt(as_column(lined) / D + epsilon)
+
+    def encode(c):
+        landed(srecv.at[c], "s", c, across)
+        scaled = (sown[c] + srecv[c]) * factor(c, CFLAT // 128)
+        enc[c] = scaled.astype(jnp.bfloat16).reshape(E, CROWS, 256)
+        for d in list(range(1, S)) + [0]:
+            dst = lax.rem(r + d, S)
+            for k in range(cap):
+                block = enc[c, pidx[0, dst * cap + k]]
+                if d:
+                    zs[c, dst, k] = block
+                else:
+                    zr[c, dst, k] = block
+            if d:
+                z_copy(c, d).start()
+
+    def place(c):
+        for d in range(1, S):
+            z_landed(c, d)
+        zl[...] = zr[c].reshape(zl.shape)
+        for l in list(range(NB_SEQ - 1, -1, -1)):
+            where = lidx[0, r * NB_SEQ + l]
+            ctx[2 + l, ctx_rows(e, c), :] = zl[where]
+        @pl.when(r < S - 1)
+        def _():
+            prior_copy(c, True).start()
+            prior_copy(c, False).start()
+        forward_copy(c).start()
+
+    def third_pass(c, carry):
+        encode(c)
+        place(c - 1)
+        return carry
+
+    encode(0)
+    lax.fori_loop(1, C, third_pass, 0)
+
+    landed(trecv, "ts", 0, across)
+    scaled = (town[...] + trecv[...]) * (factor(C, half // 128) * 128 ** (-0.5))
+    rounded = scaled.astype(jnp.bfloat16)
+    first = e == 0
+    qb[e] = jnp.where(first, rounded[:, :128], rounded[:, 128:])
+    qs[...] = jnp.where(first, rounded[:, 128:], rounded[:, :128])
+    begin(rc(qs, qb.at[e], "q", 0, partner))
+
+    place(C - 1)
+    landed(qb.at[pe], "q", 0, partner)
+
+    def settle(c, carry):
+        landed(own_rows(pe, c), "fwd", c, partner)
+
+        @pl.when(r > 0)
+        def _():
+            back = lax.rem(r + S - 1, S)
+            landed(ctx.at[pl.ds(0, 2), ctx_rows(e, c), :], "pr0", c, {"seq": back})
+            landed(ctx.at[pl.ds(0, 2), ctx_rows(pe, c), :], "pr1", c, {"seq": back, "enc": pe})
+
+        return carry
+
+    lax.fori_loop(0, C, settle, 0)
+
+    spans = half // SPAN
+
+    def attend(c, carry):
+        queries = qb[c // spans, rows(c % spans * SPAN, SPAN), :]
+        pair = ctx[pl.ds(2 * c, 2)].reshape(NBR * RLEN, 256)
+        scores = lax.dot_general(
+            queries, pair[:, :128], (((1,), (1,)), ((), ())), preferred_element_type=f32
+        )
+        raised = jnp.exp(scores - jnp.max(scores, axis=1, keepdims=True))
+        weight = (raised / jnp.sum(raised, axis=1, keepdims=True)).astype(jnp.bfloat16)
+        mixed = jnp.dot(weight, pair[:, 128:], preferred_element_type=f32)
+        out[rows(c * SPAN, SPAN), :] = mixed.astype(jnp.bfloat16)
+        return carry
+
+    lax.fori_loop(0, 2 * spans, attend, 0)
+
+    def drain(c, carry):
+        sent_chunk(c).wait_send()
+        partial_copy(c).wait_send()
+        for d in range(1, S):
+            z_copy(c, d).wait_send()
+        forward_copy(c).wait_send()
+
+        @pl.when(r < S - 1)
+        def _():
+            prior_copy(c, True).wait_send()
+            prior_copy(c, False).wait_send()
+
+        return carry
+
+    lax.fori_loop(0, C, drain, 0)
+    for copy in done:
+        copy.wait_send()
+
+
+def local_fused(tokens, nbr_feats, counts, slot_target, w_query, w_keyval):
+    S = lax.axis_size("seq")
+    cap = max(2, 2 * NB_SEQ // S)
+    K = tokens.shape[1]
+    half = tokens.shape[0] // 2
+    C = CHUNKS
+    bf, f32, i32 = jnp.bfloat16, jnp.float32, jnp.int32
+    anywhere = pl.BlockSpec(memory_space=pl.ANY)
+    vmem = pl.BlockSpec(memory_space=pltpu.VMEM)
+    return pl.pallas_call(
+        functools.partial(fused, S, cap),
+        out_shape=jax.ShapeDtypeStruct((2 * half, 128), bf),
+        in_specs=[vmem, vmem] + [anywhere] * 4,
+        out_specs=vmem,
+        scratch_shapes=[
+            pltpu.VMEM((2, C, ENC_CAP, CROWS, K), bf),
+            pltpu.VMEM((2, half, K), bf),
+            pltpu.VMEM((2, 2 * K, 256), bf),
+            pltpu.VMEM((2, 2 * K, 256), bf),
+            pltpu.VMEM((C, CFLAT, 256), f32),
+            pltpu.VMEM((C, CFLAT, 256), f32),
+            pltpu.VMEM((C, CFLAT, 256), f32),
+            pltpu.VMEM((half, 256), f32),
+            pltpu.VMEM((half, 256), f32),
+            pltpu.VMEM((half, 256), f32),
+            pltpu.VMEM((C + 1, 8, 128), f32),
+            pltpu.VMEM((C + 1, 8, 128), f32),
+            pltpu.VMEM((C, ENC_CAP, CROWS, 256), bf),
+            pltpu.VMEM((C, S, cap, CROWS, 256), bf),
+            pltpu.VMEM((C, S, cap, CROWS, 256), bf),
+            pltpu.VMEM((S * cap, CROWS, 256), bf),
+            pltpu.VMEM((NB_SEQ + 2, RLEN, 256), bf),
+            pltpu.VMEM((2, half, 128), bf),
+            pltpu.VMEM((half, 128), bf),
+            pltpu.VMEM((8, 128), i32),
+            pltpu.VMEM((S, 8, 128), i32),
+            pltpu.VMEM((8, 128), i32),
+            pltpu.VMEM((8, 128), i32),
+            pltpu.SMEM((8, 128), i32),
+            pltpu.SMEM((8, 128), i32),
+            pltpu.SemaphoreType.DMA((C + 5,)),
+            pltpu.SemaphoreType.DMA((14 + 6 * C + S + C * S,)),
+            pltpu.SemaphoreType.DMA((14 + 6 * C + S + C * S,)),
+        ],
+        compiler_params=pltpu.CompilerParams(
+            collective_id=0, has_side_effects=True, vmem_limit_bytes=56 << 20
+        ),
+    )(slot_target.reshape(1, -1), counts.reshape(1, -1), nbr_feats, tokens, w_query, w_keyval)
+
+
 def solution(mesh):
+    small = mesh.shape["mp"] == 2 and mesh.shape["groups"] == 2 and mesh.shape["seq"] <= 8
     placed = (
         P(("groups", "seq"), ("mp", "enc")),
         P(("groups", "seq"), None, ("mp", "enc")),
@@ -121,7 +515,7 @@
         P(None, ("mp", "enc")),
     )
     return jax.shard_map(
-        local,
+        local_fused if small else local,
         mesh=mesh,
         in_specs=placed,
         out_specs=P(("groups", "seq"), ("mp", "enc")),

time: 158 us -> 76 us (0.48)
  Pallas kernels: 0 us -> 73.6 us
  waiting for transfers between devices: 64.7 us -> 0 us
  blocking collectives: 28.1 us -> 0 us
  starting transfers between devices: 20.9 us -> 0 us
  matrix products: 15.5 us -> 0 us
  between operations: 13.6 us -> 0.01 us
  other arithmetic: 11 us -> 0 us
  local copies, waits for them, and re-layouts: 3.44 us -> 1.57 us
    pallas_call x0 -> x1, Pallas kernels: none -> 73.6 us  [local_fused(): pl.pallas_call(functools.partial(fused, S, cap), out_shape=jax.ShapeDtype...]
    reduce_scatter x2 -> x0, waiting for transfers between devices: 42.5 us -> none  [project_fold(): lax.psum_scatter(partial, ('mp', 'enc'), scatter_dimension=1, tiled=True)]
    all_to_all x1 -> x0, blocking collectives: 17.9 us -> none  [project_fold(): lax.all_to_all(weight, ('mp', 'enc'), split_axis=0, concat_axis=1, tiled=...]
    all_to_all x3 -> x0, waiting for transfers between devices: 17.6 us -> none  [the longest x1 17.6 us: local(): lax.all_to_all(packed, 'seq', split_axis=0, concat_axis=0, tiled=True)]
    dot_general x6 -> x0, matrix products: 15 us -> none  [the longest x2 11.3 us: project_fold(): partial = jnp.dot(flat_rows, mine, preferred_element_type=jnp.float32)]
    all_to_all x3 -> x0, starting transfers between devices: 13.8 us -> none  [the longest x1 5.21 us: local(): lax.all_to_all(sent_ids, 'seq', split_axis=0, concat_axis=0, tiled=True)]
    psum x1 -> x0, blocking collectives: 10.1 us -> none  [project_fold(): squares = lax.psum(jnp.sum(widened * widened, axis=1), ('mp', 'enc'))]
    ppermute x3 -> x0, starting transfers between devices: 7.04 us -> none  [the longest x2 6.97 us: passed_along(): return lax.ppermute(block, axis, route)]
  transfers between devices with their start and end apart: 8 -> 0, of which waited for: 4 -> 0; matrix products, arithmetic and copies ran while one was open for 12% -> 0% of each run, Pallas kernels for 0% -> 0%
where the time goes in v2:
time: 76 us; the launch traced here: 75.2 us
  Pallas kernels  73.6 us (97%)
  local copies, waits for them, and re-layouts  1.57 us (2%)
    pallas_call x1, Pallas kernels, local_fused(): pl.pallas_call(functools.partial(fused, S, cap), out_shape=jax.ShapeDtype...  73.6 us
    unnamed x1, local copies, waits for them, and re-layouts  1.57 us

profile of v2, /device:TPU:16, one launch (start us, length us, event | category | flops | bytes accessed | tf_op | source)
XLA Modules:
  0.0 75.2 jit_solution(6085096422887225455)
XLA Ops:
  0.0 73.6 %shard_map.64 = bf16[512,128]{1,0:T(8,128)(2,1)} custom-call(s32[1,24]{1,0:T(1,128)} %bitcast.2, s32[1,4]{1,0:T(1,128)} %bitcast.3, bf16[24,128,1024]{2,1,0:T(8,128)(2,1)} %feats.1, bf16[512,1024]{1,0:T(8,128)(2,1)} %tokens.1, bf16[4096,128]{1,0:T(8,128)(2,1)} %wq.1, bf16[4096,128]{1,0:T(8,128)(2,1)} %wkv.1), custom_call_target="tpu_custom_call" | custom-call | tf_op jit(solution)/shard_map/pallas_call | solution.py:466
  73.6 1.6 %copy.8 = bf16[512,128]{1,0:T(8,128)(2,1)} copy(bf16[512,128]{1,0:T(8,128)(2,1)} %shard_map.64) | data formatting | bytes 262144

commit v3 on v2

--- a/solution.py
+++ b/solution.py
@@ -136,7 +136,7 @@
     ids = {}
     total = 0
     for name, count in (
-        ("wx", 2), ("wo", 2), ("wf", 2), ("wy", 2), ("wg", 2), ("x", C), ("t", 1), ("ss", 1),
+        ("wx", 8), ("wo", 2), ("wf", 8), ("wy", 8), ("wg", 8), ("x", C), ("t", 1), ("ss", 1),
         ("s", C), ("ts", 1), ("tab", S), ("z", C * S), ("fwd", C), ("pr0", C), ("pr1", C), ("q", 1),
     ):
         ids[name] = total
@@ -180,11 +180,15 @@
         copy.start()
         done.append(copy)
 
-    def piece(k, part, side):
-        return woth.at[k, rows(part * K, K), lanes(side)]
+    Q = K // 4
+
+    def piece(k, part, i, side):
+        return woth.at[k, rows(part * K + i * Q, Q), lanes(side)]
 
     def weight_across(k):
-        begin(rc(weights[k].at[rows(2 * K * pm + K * g, K), :], piece(k, g, e), "wx", k, across))
+        for i in range(4):
+            source = weights[k].at[rows(2 * K * pm + K * g + i * Q, Q), :]
+            begin(rc(source, piece(k, g, i, e), "wx", 4 * k + i, across))
 
     def weight_local(k):
         source = weights[k].at[rows(2 * K * m, 2 * K), :]
@@ -208,7 +212,6 @@
     for c in range(C):
         sent_chunk(c).start()
         own_chunk(c).start()
-    weight_across(1)
     local_q = weight_local(1)
     local_q.start()
     begin(rc(tokens.at[rows(half * pe, half), :], tb.at[e], "t", 0, partner))
@@ -270,33 +273,36 @@
         sown[c] = product(one, two, wown, 0)
         return carry
 
-    def spread_across(k):
-        landed(piece(k, g, e), "wx", k, across)
-        begin(rc(piece(k, g, e), piece(k, g, e), "wy", k, beside))
-        begin(rc(piece(k, g, e), piece(k, g, e), "wf", k, partner))
-
-    def spread_beside(k):
-        landed(piece(k, pg, e), "wy", k, beside)
-        begin(rc(piece(k, pg, e), piece(k, pg, e), "wg", k, partner))
+    def spread_across(k, i):
+        here = piece(k, g, i, e)
+        landed(here, "wx", 4 * k + i, across)
+        begin(rc(here, here, "wy", 4 * k + i, beside))
+        begin(rc(here, here, "wf", 4 * k + i, partner))
+
+    def spread_beside(k, i):
+        here = piece(k, pg, i, e)
+        landed(here, "wy", 4 * k + i, beside)
+        begin(rc(here, here, "wg", 4 * k + i, partner))
 
     def spread_end(k):
-        landed(piece(k, g, pe), "wf", k, partner)
-        landed(piece(k, pg, pe), "wg", k, partner)
-
+        for i in range(4):
+            landed(piece(k, g, i, pe), "wf", 4 * k + i, partner)
+            landed(piece(k, pg, i, pe), "wg", 4 * k + i, partner)
+
+    spread_across(0, 0)
+    spread_across(0, 1)
     local_kv.wait()
     landed(wown.at[0, :, lanes(pe)], "wo", 0, partner)
-    spread_across(0)
-    lax.fori_loop(0, C // 2, first_pass, 0)
-    spread_beside(0)
-    spread_across(1)
-    lax.fori_loop(C // 2, C, first_pass, 0)
-    local_q.wait()
-    landed(wown.at[1, :, lanes(pe)], "wo", 1, partner)
-    local_t.wait()
-    landed(tb.at[pe], "t", 0, partner)
-    ss[C, 0 : half // 128, :] = as_rows(squares(tb[0]) + squares(tb[1]))
-    begin(rc(ss, ssr, "ss", 0, across))
-    spread_beside(1)
+    lax.fori_loop(0, 1, first_pass, 0)
+    spread_across(0, 2)
+    spread_across(0, 3)
+    weight_across(1)
+    spread_beside(0, 0)
+    spread_beside(0, 1)
+    lax.fori_loop(1, 2, first_pass, 0)
+    spread_beside(0, 2)
+    spread_beside(0, 3)
+    lax.fori_loop(2, C, first_pass, 0)
     spread_end(0)
 
     def partial_copy(c):
@@ -308,11 +314,23 @@
         partial_copy(c).start()
         return carry
 
-    lax.fori_loop(0, C, second_pass, 0)
+    lax.fori_loop(0, 2, second_pass, 0)
+    local_t.wait()
+    landed(tb.at[pe], "t", 0, partner)
+    ss[C, 0 : half // 128, :] = as_rows(squares(tb[0]) + squares(tb[1]))
+    begin(rc(ss, ssr, "ss", 0, across))
+    for c in range(2, C):
+        one, two = chunk_rows(c)
+        ssend[c] = product(one, two, woth, 0)
+    local_q.wait()
+    landed(wown.at[1, :, lanes(pe)], "wo", 1, partner)
+    town[...] = product(tb[0], tb[1], wown, 1)
+    for i in range(4):
+        spread_across(1, i)
+    for i in range(4):
+        spread_beside(1, i)
     spread_end(1)
     tsend[...] = product(tb[0], tb[1], woth, 1)
-    begin(rc(tsend, trecv, "ts", 0, across))
-    town[...] = product(tb[0], tb[1], wown, 1)
 
     for d in range(1, S):
         landed(tabr.at[d], "tab", d, zdev(d))
@@ -361,6 +379,15 @@
 
     def encode(c):
         landed(srecv.at[c], "s", c, across)
+
+        @pl.when(c + 2 < C)
+        def _():
+            partial_copy(c + 2).start()
+
+        @pl.when(c + 2 == C)
+        def _():
+            rc(tsend, trecv, "ts", 0, across).start()
+
         scaled = (sown[c] + srecv[c]) * factor(c, CFLAT // 128)
         enc[c] = scaled.astype(jnp.bfloat16).reshape(E, CROWS, 256)
         for d in list(range(1, S)) + [0]:
@@ -421,7 +448,7 @@
 
     spans = half // SPAN
 
-    def attend(c, carry):
+    def attend(c):
         queries = qb[c // spans, rows(c % spans * SPAN, SPAN), :]
         pair = ctx[pl.ds(2 * c, 2)].reshape(NBR * RLEN, 256)
         scores = lax.dot_general(
@@ -431,9 +458,9 @@
         weight = (raised / jnp.sum(raised, axis=1, keepdims=True)).astype(jnp.bfloat16)
         mixed = jnp.dot(weight, pair[:, 128:], preferred_element_type=f32)
         out[rows(c * SPAN, SPAN), :] = mixed.astype(jnp.bfloat16)
-        return carry
-
-    lax.fori_loop(0, 2 * spans, attend, 0)
+
+    for c in range(2 * spans):
+        attend(c)
 
     def drain(c, carry):
         sent_chunk(c).wait_send()
@@ -450,6 +477,7 @@
         return carry
 
     lax.fori_loop(0, C, drain, 0)
+    rc(tsend, trecv, "ts", 0, across).wait_send()
     for copy in done:
         copy.wait_send()
 
@@ -495,8 +523,8 @@
             pltpu.SMEM((8, 128), i32),
             pltpu.SMEM((8, 128), i32),
             pltpu.SemaphoreType.DMA((C + 5,)),
-            pltpu.SemaphoreType.DMA((14 + 6 * C + S + C * S,)),
-            pltpu.SemaphoreType.DMA((14 + 6 * C + S + C * S,)),
+            pltpu.SemaphoreType.DMA((38 + 6 * C + S + C * S,)),
+            pltpu.SemaphoreType.DMA((38 + 6 * C + S + C * S,)),
         ],
         compiler_params=pltpu.CompilerParams(
             collective_id=0, has_side_effects=True, vmem_limit_bytes=56 << 20

time: 76 us -> 70.5 us (0.928)
  Pallas kernels: 73.6 us -> 67.9 us
    pallas_call x1, Pallas kernels: 73.6 us -> 67.9 us  [local_fused(): pl.pallas_call(functools.partial(fused, S, cap), out_shape=jax.ShapeDtype...]
where the time goes in v3:
time: 70.5 us; the launch traced here: 69.4 us
  Pallas kernels  67.9 us (96%)
  local copies, waits for them, and re-layouts  1.57 us (2%)
    pallas_call x1, Pallas kernels, local_fused(): pl.pallas_call(functools.partial(fused, S, cap), out_shape=jax.ShapeDtype...  67.9 us
    unnamed x1, local copies, waits for them, and re-layouts  1.57 us

profile of v3, /device:TPU:16, one launch (start us, length us, event | category | flops | bytes accessed | tf_op | source)
XLA Modules:
  0.0 69.4 jit_solution(14726619522906043284)
XLA Ops:
  0.0 67.9 %shard_map.64 = bf16[512,128]{1,0:T(8,128)(2,1)} custom-call(s32[1,24]{1,0:T(1,128)} %bitcast.2, s32[1,4]{1,0:T(1,128)} %bitcast.3, bf16[24,128,1024]{2,1,0:T(8,128)(2,1)} %feats.1, bf16[512,1024]{1,0:T(8,128)(2,1)} %tokens.1, bf16[4096,128]{1,0:T(8,128)(2,1)} %wq.1, bf16[4096,128]{1,0:T(8,128)(2,1)} %wkv.1), custom_call_target="tpu_custom_call" | custom-call | tf_op jit(solution)/shard_map/pallas_call | solution.py:494
  67.9 1.6 %copy.8 = bf16[512,128]{1,0:T(8,128)(2,1)} copy(bf16[512,128]{1,0:T(8,128)(2,1)} %shard_map.64) | data formatting | bytes 262144
